TPU v7x, 512 devices: a whole 4x8x8 slice. The times are simulated.
512 devices in a mesh: frames: 64 (over x, y, core), cols: 8 (over z).
Axes of the slice: x: 4, y: 8, z: 8, core: 2. Of those that a mesh axis runs over, the one named last changes fastest.
Arguments:
- panel: float32 [32768, 512], P('frames', 'cols'), may hold values from -12 to 12
- trailing: float32 [32768, 4096], P('frames', 'cols'), may hold values from -6 to 6
Outputs:
- r_factor: float32 [512, 512], P('frames')
- coupling: float32 [512, 4096], P('frames', 'cols')
- remainder: float32 [32768, 4096], P('frames', 'cols')
All inputs are finite; a program needn't handle non-finite values.
Results may differ from a plain program's by a relative error of at most 0.0003.
Values sent between devices are 32-bit elements; how exact they have to be, the bound alone decides.
A program may use at most 64 MiB of HBM per device.

v0:
```python
import jax
import jax.numpy as jnp
from jax import lax
from jax.sharding import PartitionSpec as P


def partner_2(value, axis, stride):
    mask = 2**stride
    pairs = [(source, source ^ mask) for source in range(lax.axis_size(axis))]
    return lax.ppermute(value, axis, pairs)


def body(panel, trailing):
    highest = lax.Precision.HIGHEST
    row_block = lax.all_gather(panel, "cols", axis=1, tiled=True)
    gram = jnp.dot(row_block.T, row_block, precision=highest, preferred_element_type=jnp.float32)
    levels = lax.axis_size("frames").bit_length() - 1
    for level in range(levels):
        partner = partner_2(gram, "frames", level)
        gram = gram + partner
    lower = jnp.linalg.cholesky(gram)
    upper = lower.T
    basis_t = jax.scipy.linalg.solve_triangular(lower, row_block.T, lower=True)
    local_term = jnp.dot(basis_t, trailing, precision=highest, preferred_element_type=jnp.float32)
    coupling = lax.psum(local_term, "frames")
    remainder = trailing - jnp.dot(
        basis_t.T, coupling, precision=highest, preferred_element_type=jnp.float32
    )
    height = upper.shape[0] // lax.axis_size("frames")
    offset = lax.axis_index("frames") * height
    r_rows = lax.dynamic_slice_in_dim(upper, offset, height, 0)
    coupling_rows = lax.dynamic_slice_in_dim(coupling, offset, height, 0)
    return (r_rows, coupling_rows, remainder)


def solution(mesh):
    placed = (P("frames", "cols"), P("frames", "cols"))
    return jax.shard_map(
        body,
        mesh=mesh,
        in_specs=placed,
        out_specs=(P("frames", None), P("frames", "cols"), P("frames", "cols")),
        check_vma=False,
    )
```

profile of v0, /device:TPU:1, one launch (start us, length us, event | category | flops | bytes accessed | tf_op | source)
XLA Modules:
  0.0 597.8 jit_solution(14355997508250597249)
XLA Ops:
  7.2 0.7 all-gather.2.cloned.1.call-update
  7.9 44.9 %all-gather.2.cloned.1.call-done = f32[512,512]{0,1:T(8,128)} async-done(((f32[512,64]{0,1:T(8,128)}), f32[512,512]{0,1:T(8,128)}) %all-gather.2.cloned.1.call-update) | async-done | bytes 1048592 | tf_op jit(solution)/shard_map/all_gather | solution.py:15
  52.8 3.4 fusion.40
  56.2 7.2 %collective-permute-start = (f32[512,512]{0,1:T(8,128)S(1)}, f32[512,512]{0,1:T(8,128)S(1)}, u32[]{:S(2)}, u32[]{:S(2)}) collective-permute-start(f32[512,512]{0,1:T(8,128)S(1)} %fusion.40), channel_id=1, source_target_pairs={{0,8},{8,0},{16,24},{24,16},{32,40},{40,32},{48,56},{56,48},{64,72... | collective-permute-start | bytes 3145736 | tf_op jit(solution)/shard_map/ppermute | solution.py:10
  63.4 2.3 collective-permute-done
  65.9 3.1 collective-permute-start.1
  69.0 23.1 %collective-permute-done.1 = f32[512,512]{0,1:T(8,128)S(1)} collective-permute-done((f32[512,512]{0,1:T(8,128)S(1)}, f32[512,512]{0,1:T(8,128)S(1)}, u32[]{:S(2)}, u32[]{:S(2)}) %collective-permute-start.1) | collective-permute-done | bytes 1048608 | tf_op jit(solution)/shard_map/ppermute | solution.py:10
  92.4 4.0 collective-permute-start.2
  96.4 45.4 %collective-permute-done.2 = f32[512,512]{0,1:T(8,128)S(1)} collective-permute-done((f32[512,512]{0,1:T(8,128)S(1)}, f32[512,512]{0,1:T(8,128)S(1)}, u32[]{:S(2)}, u32[]{:S(2)}) %collective-permute-start.2) | collective-permute-done | bytes 1048608 | tf_op jit(solution)/shard_map/ppermute | solution.py:10
  142.0 8.0 %collective-permute-start.3 = (f32[512,512]{0,1:T(8,128)S(1)}, f32[512,512]{0,1:T(8,128)S(1)}, u32[]{:S(2)}, u32[]{:S(2)}) collective-permute-start(f32[512,512]{0,1:T(8,128)S(1)} %add.67), channel_id=1, source_target_pairs={{0,64},{8,72},{16,80},{24,88},{32,96},{40,104},{48,112},{56,120},{... | collective-permute-start | bytes 3145736 | tf_op jit(solution)/shard_map/ppermute | solution.py:10
  150.0 45.4 %collective-permute-done.3 = f32[512,512]{0,1:T(8,128)S(1)} collective-permute-done((f32[512,512]{0,1:T(8,128)S(1)}, f32[512,512]{0,1:T(8,128)S(1)}, u32[]{:S(2)}, u32[]{:S(2)}) %collective-permute-start.3) | collective-permute-done | bytes 1048608 | tf_op jit(solution)/shard_map/ppermute | solution.py:10
  195.7 3.1 collective-permute-start.4
  198.7 21.9 %collective-permute-done.4 = f32[512,512]{0,1:T(8,128)S(1)} collective-permute-done((f32[512,512]{0,1:T(8,128)S(1)}, f32[512,512]{0,1:T(8,128)S(1)}, u32[]{:S(2)}, u32[]{:S(2)}) %collective-permute-start.4) | collective-permute-done | bytes 1048608 | tf_op jit(solution)/shard_map/ppermute | solution.py:10
  220.9 5.1 collective-permute-start.5
  226.0 20.6 %collective-permute-done.5 = f32[512,512]{0,1:T(8,128)S(1)} collective-permute-done((f32[512,512]{0,1:T(8,128)S(1)}, f32[512,512]{0,1:T(8,128)S(1)}, u32[]{:S(2)}, u32[]{:S(2)}) %collective-permute-start.5) | collective-permute-done | bytes 1048608 | tf_op jit(solution)/shard_map/ppermute | solution.py:10
  247.3 11.7 %cholesky.104 = f32[128,128]{1,0:T(8,128)S(1)} custom-call(f32[128,128]{1,0:T(8,128)S(1)} %cholesky.266), custom_call_target="Cholesky" | custom-call | tf_op jit(solution)/shard_map/jit(cholesky)/cholesky | solution.py:21
  259.1 9.8 %custom-call.31 = f32[1,128,128]{1,2,0:T(8,128)S(1)} custom-call(f32[1,128,128]{2,1,0:T(8,128)S(1)} %get-tuple-element.35), custom_call_target="InvertDiagBlocksLowerTriangular" | custom-call | tf_op jit(solution)/shard_map/jit(cholesky)/cholesky | solution.py:21
  269.4 0.5 slice_subtract_fusion
  270.1 11.7 %cholesky.217 = f32[128,128]{1,0:T(8,128)S(1)} custom-call(f32[128,128]{1,0:T(8,128)S(1)} %cholesky.270), custom_call_target="Cholesky" | custom-call | tf_op jit(solution)/shard_map/jit(cholesky)/cholesky | solution.py:21
  281.9 10.0 %custom-call.32 = f32[1,128,128]{1,2,0:T(8,128)S(1)} custom-call(f32[1,128,128]{2,1,0:T(8,128)S(1)} %get-tuple-element.32), custom_call_target="InvertDiagBlocksLowerTriangular" | custom-call | tf_op jit(solution)/shard_map/jit(cholesky)/cholesky | solution.py:21
  292.5 11.7 %cholesky.238 = f32[128,128]{1,0:T(8,128)S(1)} custom-call(f32[128,128]{1,0:T(8,128)S(1)} %cholesky.275), custom_call_target="Cholesky" | custom-call | tf_op jit(solution)/shard_map/jit(cholesky)/cholesky | solution.py:21
  304.2 0.6 compare_reduce_fusion.1
  304.9 9.8 %custom-call.33 = f32[1,128,128]{1,2,0:T(8,128)S(1)} custom-call(f32[1,128,128]{2,1,0:T(8,128)S(1)} %get-tuple-element.29), custom_call_target="InvertDiagBlocksLowerTriangular" | custom-call | tf_op jit(solution)/shard_map/jit(cholesky)/cholesky | solution.py:21
  315.3 11.9 %cholesky.255 = f32[128,128]{1,0:T(8,128)S(1)} custom-call(f32[128,128]{1,0:T(8,128)S(1)} %slice_subtract_fusion.2), custom_call_target="Cholesky" | custom-call | tf_op jit(solution)/shard_map/jit(cholesky)/cholesky | solution.py:21
  327.2 0.6 compare_reduce_fusion
  327.9 0.6 compare_reduce_fusion.2
  331.0 1.2 fusion.1
  332.3 10.4 %while.1 = (s32[]{:T(128)}, f32[512,512]{1,0:T(8,128)S(1)}, s32[4,2]{0,1:T(2,128)S(1)}, f32[4,128,128]{2,1,0:T(8,128)}, s32[]{:T(128)}) while((s32[]{:T(128)}, f32[512,512]{1,0:T(8,128)S(1)}, s32[4,2]{0,1:T(2,128)S(1)}, f32[4,128,128]{2,1,0:T(8,128)}, s32[]{:T(128)}) %tuple.32), condition=%wide.while_cond, body=%wide.while_body.sunk | while | flops 2 | bytes 132705 | solution.py:23
  332.3 0.5 fusion.51
  332.9 2.0 bitcast_dynamic-update-slice_fusion.2
  334.9 0.5 fusion.51
  335.5 2.0 bitcast_dynamic-update-slice_fusion.2
  337.5 0.5 fusion.51
  338.1 2.0 bitcast_dynamic-update-slice_fusion.2
  340.1 0.5 fusion.51
  340.7 2.0 bitcast_dynamic-update-slice_fusion.2
  342.7 40.2 %custom-call.34 = f32[4,128,128]{1,2,0:T(8,128)S(1)} custom-call(f32[4,128,128]{2,1,0:T(8,128)} %get-tuple-element.10), custom_call_target="InvertDiagBlocksLowerTriangular" | custom-call | tf_op jit(solution)/shard_map/jit(_solve_triangular)/triangular_solve | solution.py:23
  382.8 0.4 fusion.11
  384.1 0.4 convolution_subtract_fusion.1
  384.5 0.4 fusion.24
  385.0 1.6 convolution_subtract_fusion.3
  386.6 0.4 fusion.23
  387.1 2.9 fusion.7
  390.0 1.1 dynamic-slice_bitcast_fusion
  391.1 0.7 copy.11
  391.8 193.6 %all-reduce.3.cloned.1.call-done = f32[512,512]{1,0:T(8,128)} async-done(((f32[512,512]{1,0:T(8,128)}), f32[512,512]{1,0:T(8,128)}) %all-reduce.3.cloned.1.call-update) | async-done | bytes 1048592 | tf_op jit(solution)/shard_map/psum | solution.py:25
  585.3 4.0 convolution_subtract_fusion
  589.4 1.3 constant_dynamic-slice_fusion.1
  (41 shorter events, 5.1 us)
Async XLA Ops:
  7.2 45.7 %all-gather.2.cloned.1.call-start = ((), (), s32[]{:S(2)}) async-start(), calls=%async_computation | async-start | bytes 1179648 | tf_op jit(solution)/shard_map/all_gather | solution.py:15
  7.9 577.4 %all-reduce.3.cloned.1.call-start = ((), (), s32[]{:S(2)}) async-start(), calls=%async_computation.1 | async-start | bytes 2097152 | tf_op jit(solution)/shard_map/psum | solution.py:25
  56.2 9.5 %collective-permute-start = (f32[512,512]{0,1:T(8,128)S(1)}, f32[512,512]{0,1:T(8,128)S(1)}, u32[]{:S(2)}, u32[]{:S(2)}) collective-permute-start(f32[512,512]{0,1:T(8,128)S(1)} %fusion.40), channel_id=1, source_target_pairs={{0,8},{8,0},{16,24},{24,16},{32,40},{40,32},{48,56},{56,48},{64,72... | collective-permute-start | bytes 3145736 | tf_op jit(solution)/shard_map/ppermute | solution.py:10
  65.9 26.2 %collective-permute-start.1 = (f32[512,512]{0,1:T(8,128)S(1)}, f32[512,512]{0,1:T(8,128)S(1)}, u32[]{:S(2)}, u32[]{:S(2)}) collective-permute-start(f32[512,512]{0,1:T(8,128)S(1)} %add.65), channel_id=1, source_target_pairs={{0,16},{8,24},{16,0},{24,8},{32,48},{40,56},{48,32},{56,40},{64,80... | collective-permute-start | bytes 3145736 | tf_op jit(solution)/shard_map/ppermute | solution.py:10
  92.4 49.4 %collective-permute-start.2 = (f32[512,512]{0,1:T(8,128)S(1)}, f32[512,512]{0,1:T(8,128)S(1)}, u32[]{:S(2)}, u32[]{:S(2)}) collective-permute-start(f32[512,512]{0,1:T(8,128)S(1)} %add.66), channel_id=1, source_target_pairs={{0,32},{8,40},{16,48},{24,56},{32,0},{40,8},{48,16},{56,24},{64,96... | collective-permute-start | bytes 3145736 | tf_op jit(solution)/shard_map/ppermute | solution.py:10
  142.0 53.4 %collective-permute-start.3 = (f32[512,512]{0,1:T(8,128)S(1)}, f32[512,512]{0,1:T(8,128)S(1)}, u32[]{:S(2)}, u32[]{:S(2)}) collective-permute-start(f32[512,512]{0,1:T(8,128)S(1)} %add.67), channel_id=1, source_target_pairs={{0,64},{8,72},{16,80},{24,88},{32,96},{40,104},{48,112},{56,120},{... | collective-permute-start | bytes 3145736 | tf_op jit(solution)/shard_map/ppermute | solution.py:10
  195.7 25.0 %collective-permute-start.4 = (f32[512,512]{0,1:T(8,128)S(1)}, f32[512,512]{0,1:T(8,128)S(1)}, u32[]{:S(2)}, u32[]{:S(2)}) collective-permute-start(f32[512,512]{0,1:T(8,128)S(1)} %add.68), channel_id=1, source_target_pairs={{0,128},{8,136},{16,144},{24,152},{32,160},{40,168},{48,176},{56,1... | collective-permute-start | bytes 3145736 | tf_op jit(solution)/shard_map/ppermute | solution.py:10
  220.9 25.7 %collective-permute-start.5 = (f32[512,512]{0,1:T(8,128)S(1)}, f32[512,512]{0,1:T(8,128)S(1)}, u32[]{:S(2)}, u32[]{:S(2)}) collective-permute-start(f32[512,512]{0,1:T(8,128)S(1)} %add.69), channel_id=1, source_target_pairs={{0,256},{8,264},{16,272},{24,280},{32,288},{40,296},{48,304},{56,3... | collective-permute-start | bytes 3145736 | tf_op jit(solution)/shard_map/ppermute | solution.py:10
  331.0 51.8 %copy-start = (f32[512,512]{0,1:T(8,128)S(1)}, f32[512,512]{0,1:T(8,128)}, u32[]{:S(2)}) copy-start(f32[512,512]{0,1:T(8,128)} %all-gather.2.cloned.1.call-done) | copy-start | bytes 3145732
  342.7 41.9 %copy-start.2 = (f32[512,512]{1,0:T(8,128)}, f32[512,512]{1,0:T(8,128)S(1)}, u32[]{:S(2)}) copy-start(f32[512,512]{1,0:T(8,128)S(1)} %get-tuple-element.93) | copy-start | bytes 3145732
  384.9 2.1 copy-start.1
Sparse Core Ops, SparseCore 0:
  10.1 42.7 all-gather.1
  390.1 195.2 all-reduce.2
where the time goes:
time: 603 us; the launch traced here: 598 us
  waiting for transfers between devices  398 us (66%)
  other arithmetic  122 us (20%)
  starting transfers between devices  30.6 us (5%)
  between operations  17.1 us (3%)
  matrix products  16.6 us (3%)
  local copies, waits for them, and re-layouts  14.1 us (2%)
    psum x1, waiting for transfers between devices, body(): coupling = lax.psum(local_term, 'frames')  194 us
    ppermute x6, waiting for transfers between devices, partner_2(): return lax.ppermute(value, axis, pairs)  159 us
    another operation x14, other arithmetic, body(): lower = jnp.linalg.cholesky(gram)  78.7 us
    all_gather x1, waiting for transfers between devices, body(): row_block = lax.all_gather(panel, 'cols', axis=1, tiled=True)  44.9 us
    another operation x3, other arithmetic, body(): basis_t = jax.scipy.linalg.solve_triangular(lower, row_block.T, lower=True)  41.4 us
    ppermute x6, starting transfers between devices, partner_2(): return lax.ppermute(value, axis, pairs)  30.5 us
  transfers between devices with their start and end apart: 8, of which 8 were waited for; matrix products, arithmetic and copies ran while one was open for 0% of the time, Pallas kernels for 0%

commit v1 on v0

v1 whole, which is shorter than its diff:
```python
import functools

import jax
import jax.numpy as jnp
from jax import lax
from jax.experimental import pallas as pl
from jax.experimental.pallas import tpu as pltpu
from jax.sharding import PartitionSpec as P

HI = lax.Precision.HIGHEST
F32 = jnp.float32
MESH = pl.DeviceIdType.MESH


def frame_dims(frames):
    return {64: (4, 8, 2), 8: (2, 2, 2)}[frames]


def sum_slots(ref):
    total = ref[0]
    for slot in range(1, ref.shape[0]):
        total = total + ref[slot]
    return total


def reduce_kernel(
    dims, panel_ref, trail_ref, rt_ref, g_ref, c_ref,
    gp, gcore, gs, gx, gy, xs, xo, xcore, xx, xr, xy,
    ring_send, ring_recv, core_send, core_recv, x_send, x_recv, y_send, y_recv, z_send, z_recv,
):
    nx, ny, nq, nz = dims
    f = lax.axis_index("frames")
    z = lax.axis_index("cols")
    q = lax.rem(f, nq)
    y = lax.rem(f // nq, ny)
    x = f // (nq * ny)

    def device(x=x, y=y, q=q, z=z):
        return ((x * ny + y) * nq + q, z)

    def step(me, d, n):
        return lax.rem(me + d, n)

    partners = [device(q=step(q, d, nq)) for d in range(1, nq)]
    partners += [device(x=step(x, d, nx)) for d in range(1, nx)]
    partners += [device(y=step(y, d, ny)) for d in range(1, ny)]
    partners += [device(z=step(z, d, nz)) for d in range(1, nz)]
    barrier = pltpu.get_barrier_semaphore()
    for other in partners:
        pl.semaphore_signal(barrier, inc=1, device_id=other, device_id_type=MESH)
    width = panel_ref.shape[1]
    rt_ref[pl.ds(pl.multiple_of(z * width, width), width), :] = panel_ref[...].T
    pl.semaphore_wait(barrier, len(partners))

    pending = []

    def push(src, dst, send, recv, to):
        copy = pltpu.make_async_remote_copy(
            src_ref=src, dst_ref=dst, send_sem=send, recv_sem=recv, device_id=to, device_id_type=MESH
        )
        copy.start()
        pending.append(copy)
        return copy

    def arrived(copies):
        for copy in copies:
            copy.wait_recv()

    half = width // 2
    last = nz // 2 - 1
    moving = {}
    for s in range(nz // 2):
        for piece in range(2):
            for way in range(2):
                if s == last and piece != way:
                    continue
                if s > 0:
                    moving[s - 1, piece, way].wait_recv()
                owner = lax.rem(z + nz - s, nz) if way == 0 else lax.rem(z + s, nz)
                there = step(z, 1, nz) if way == 0 else step(z, nz - 1, nz)
                block = rt_ref.at[pl.ds(pl.multiple_of(owner * width + piece * half, half), half), :]
                moving[s, piece, way] = push(
                    block, block, ring_send.at[way, s, piece], ring_recv.at[way, s, piece], device(z=there)
                )
    waited = {key for key in moving if (key[0] + 1, key[1], key[2]) in moving}
    for key in moving:
        if key not in waited:
            moving[key].wait_recv()

    own = rt_ref[pl.ds(pl.multiple_of(z * width, width), width), :]
    gp[...] = lax.dot_general(
        own, rt_ref[...], (((1,), (1,)), ((), ())), precision=HI, preferred_element_type=F32
    ).reshape(gp.shape)
    other_q = step(q, 1, nq)
    core = device(q=other_q)
    g_core = [push(gp.at[other_q], gcore, core_send.at[0], core_recv.at[0], core)]

    rows = rt_ref.shape[0] // nq

    def cross(part):
        left = rt_ref[pl.ds(pl.multiple_of(part * rows, rows), rows), :]
        return jnp.dot(left, trail_ref[...], precision=HI, preferred_element_type=F32).reshape(xs.shape)

    xs[...] = cross(other_q)
    x_core = [push(xs, xcore, core_send.at[1], core_recv.at[1], core)]
    xo[...] = cross(q)

    arrived(g_core)
    gs[...] = gp[q] + gcore[...]
    gx[x] = gs[x]

    def along_x(stage, src, dst):
        return [
            push(src(step(x, d, nx)), dst, x_send.at[stage, d], x_recv.at[stage, d], device(x=step(x, d, nx)))
            for d in range(1, nx)
        ]

    def along_y(stage, src, dst):
        return [
            push(src(step(y, d, ny)), dst, y_send.at[stage, d], y_recv.at[stage, d], device(y=step(y, d, ny)))
            for d in range(1, ny)
        ]

    g_x = along_x(0, lambda to: gs.at[to], gx.at[x])
    arrived(x_core)
    xo[...] = xo[...] + xcore[...]
    xx[x] = xo[x]
    x_x = along_x(1, lambda to: xo.at[to], xx.at[x])
    arrived(g_x)
    gy[y] = sum_slots(gx)
    g_y = along_y(0, lambda to: gy.at[y], gy.at[y])
    arrived(x_x)
    xr[...] = sum_slots(xx)
    xy[y] = xr[y]
    x_y = along_y(1, lambda to: xr.at[to], xy.at[y])
    arrived(g_y)
    g_ref[z, q, x] = sum_slots(gy)
    piece = g_ref.at[z, q, x]
    g_z = [
        push(piece, piece, z_send.at[d], z_recv.at[d], device(z=step(z, d, nz))) for d in range(1, nz)
    ]
    arrived(x_y)
    c_ref[q, x, y] = sum_slots(xy)
    x_y = along_y(2, lambda to: c_ref.at[q, x, y], c_ref.at[q, x, y])
    arrived(g_z)
    g_x = along_x(2, lambda to: g_ref.at[:, q, x], g_ref.at[:, q, x])
    arrived(x_y)
    x_x = along_x(3, lambda to: c_ref.at[q, x], c_ref.at[q, x])
    arrived(g_x)
    g_core = [push(g_ref.at[:, q], g_ref.at[:, q], core_send.at[2], core_recv.at[2], core)]
    arrived(x_x)
    x_core = [push(c_ref.at[q], c_ref.at[q], core_send.at[3], core_recv.at[3], core)]
    arrived(g_core)
    arrived(x_core)
    for copy in pending:
        copy.wait_send()


def reduce_products(dims, panel, trail):
    nx, ny, nq, nz = dims
    height, width = panel.shape
    cols = trail.shape[1]
    n = width * nz
    rg = n // (nz * nq * nx)
    rx = n // (nq * nx * ny)
    vm = pl.BlockSpec(memory_space=pltpu.VMEM)
    dma = pltpu.SemaphoreType.DMA
    rt, g, c = pl.pallas_call(
        functools.partial(reduce_kernel, dims),
        out_shape=(
            jax.ShapeDtypeStruct((n, height), F32),
            jax.ShapeDtypeStruct((nz, nq, nx, rg, n), F32),
            jax.ShapeDtypeStruct((nq, nx, ny, rx, cols), F32),
        ),
        in_specs=[vm, vm],
        out_specs=(vm,) * 3,
        scratch_shapes=[
            pltpu.VMEM((nq, nx, rg, n), F32),
            pltpu.VMEM((nx, rg, n), F32),
            pltpu.VMEM((nx, rg, n), F32),
            pltpu.VMEM((nx, rg, n), F32),
            pltpu.VMEM((ny, rg, n), F32),
            pltpu.VMEM((nx, ny, rx, cols), F32),
            pltpu.VMEM((nx, ny, rx, cols), F32),
            pltpu.VMEM((nx, ny, rx, cols), F32),
            pltpu.VMEM((nx, ny, rx, cols), F32),
            pltpu.VMEM((ny, rx, cols), F32),
            pltpu.VMEM((ny, rx, cols), F32),
            dma((2, nz // 2, 2)), dma((2, nz // 2, 2)),
            dma((4,)), dma((4,)),
            dma((4, nx)), dma((4, nx)),
            dma((3, ny)), dma((3, ny)),
            dma((nz,)), dma((nz,)),
        ],
        compiler_params=pltpu.CompilerParams(
            collective_id=0, has_side_effects=True, vmem_limit_bytes=40 * 2**20
        ),
        name="reduce_products",
    )(panel, trail)
    return rt, g.reshape(n, n), c.reshape(n, cols)


def split3(v):
    h = v.astype(jnp.bfloat16).astype(F32)
    rest = v - h
    m = rest.astype(jnp.bfloat16).astype(F32)
    low = rest - m
    return h, m, low

def lane(v, c):
    return jnp.broadcast_to(v[:, c:c + 1], v.shape)

def factor_block(s_ref, m_ref):
    n = s_ref.shape[0]
    steps = n // 8
    sub = lax.broadcasted_iota(jnp.int32, (8, n), 0)
    col = lax.broadcasted_iota(jnp.int32, (8, n), 1)
    x = [jnp.broadcast_to(s_ref[i:i + 1, :], (8, n)) for i in range(8)]
    d = [[lane(x[i], k) for k in range(i + 1)] for i in range(8)]
    for j in range(steps):
        base = 8 * j
        own = (col >= base) & (col < base + 8)
        x = [jnp.where(own, jnp.where(col == base + i, 1.0, 0.0), x[i]) for i in range(8)]
        u = []
        low = [[None] * 8 for _ in range(8)]
        for k in range(8):
            scale = lax.rsqrt(d[k][k])
            for i in range(k + 1, 8):
                low[i][k] = d[i][k] * scale
            for i in range(k + 1, 8):
                for m in range(k + 1, i + 1):
                    d[i][m] = d[i][m] - low[i][k] * low[m][k]
            u.append(x[k] * scale)
            for i in range(k + 1, 8):
                x[i] = x[i] - low[i][k] * u[k]
        packed = u[7]
        for k in range(7):
            packed = jnp.where(sub == k, u[k], packed)
        m_ref[base:base + 8, :] = jnp.where(col < base + 8, packed, 0.0)
        if j == steps - 1:
            break
        nxt = base + 8
        if j + 2 < steps:
            h, mid, lo = split3(packed)
            left = jnp.concatenate([h, h, mid, mid, h, lo], axis=0).astype(jnp.bfloat16)
            right = jnp.concatenate([h, mid, h, mid, lo, h], axis=0).astype(jnp.bfloat16)
            update = lax.dot_general(left, right, (((0,), (0,)), ((), ())), preferred_element_type=F32)
        x = [jnp.broadcast_to(s_ref[nxt + i:nxt + i + 1, :], (8, n)) for i in range(8)]
        d = [[lane(x[i], nxt + k) for k in range(i + 1)] for i in range(8)]
        x = [jnp.where(own, 0.0, v) for v in x]
        for k in range(8):
            w = [lane(u[k], nxt + i) for i in range(8)]
            for i in range(8):
                x[i] = x[i] - w[i] * u[k]
                for m in range(i + 1):
                    d[i][m] = d[i][m] - w[i] * w[m]
        if j + 2 < steps:
            for p in range(j + 2, steps):
                s_ref[8 * p:8 * p + 8, :] = jnp.where(own, 0.0, s_ref[8 * p:8 * p + 8, :]) - update[8 * p:8 * p + 8, :]

def finish_kernel(nb, g_ref, c_ref, rt_ref, t_ref, r_out, c_out, rem_out, s, v, r, blk, inv):
    n = g_ref.shape[0]
    b = n // nb
    s[...] = g_ref[...]
    rowb = lax.broadcasted_iota(jnp.int32, (n, n), 0) // b
    colb = lax.broadcasted_iota(jnp.int32, (n, n), 1) // b
    rowcol = lax.broadcasted_iota(jnp.int32, (b, n), 1)
    rowrow = lax.broadcasted_iota(jnp.int32, (b, n), 0)
    @pl.loop(0, nb)
    def _(step):
        off = pl.multiple_of(step * b, b)
        blk[...] = s[pl.ds(off, b), pl.ds(off, b)]
        factor_block(blk, inv)
        y = jnp.dot(inv[...], s[pl.ds(off, b), :], precision=HI, preferred_element_type=F32)
        r[pl.ds(off, b), :] = jnp.where(rowcol >= rowrow + off, y, 0.0)
        v[pl.ds(off, b), :] = jnp.where(rowcol < off, y, 0.0)
        v[pl.ds(off, b), pl.ds(off, b)] = inv[...]
        coef = jnp.where(rowcol >= off + b, y, 0.0)
        own = jnp.where(rowcol >= off + b, y, v[pl.ds(off, b), :])
        upd = lax.dot_general(coef, own, (((0,), (0,)), ((), ())), precision=HI, preferred_element_type=F32)
        s[...] = jnp.where((colb == step) & (rowb > step), 0.0, s[...]) - upd
    coup = jnp.dot(v[...], c_ref[...], precision=HI, preferred_element_type=F32)
    s[...] = coup
    w = lax.dot_general(v[...], coup, (((0,), (0,)), ((), ())), precision=HI, preferred_element_type=F32)
    rem_out[...] = t_ref[...] - lax.dot_general(rt_ref[...], w, (((0,), (0,)), ((), ())), precision=HI, preferred_element_type=F32)
    height = r_out.shape[0]
    pos = pl.multiple_of(lax.axis_index("frames") * height, height)
    r_out[...] = r[pl.ds(pos, height), :]
    c_out[...] = s[pl.ds(pos, height), :]

def finish(g, c, rt, t, height, nb=4):
    n, m = c.shape
    b = n // nb
    vm = pl.BlockSpec(memory_space=pltpu.VMEM)
    return pl.pallas_call(
        functools.partial(finish_kernel, nb),
        out_shape=(jax.ShapeDtypeStruct((height, n), F32), jax.ShapeDtypeStruct((height, m), F32), jax.ShapeDtypeStruct(t.shape, F32)),
        in_specs=[vm] * 4, out_specs=(vm,) * 3,
        scratch_shapes=[pltpu.VMEM((n, n), F32)] * 3 + [pltpu.VMEM((b, b), F32)] * 2,
        compiler_params=pltpu.CompilerParams(vmem_limit_bytes=48 * 2**20),
        name="finish",
    )(g, c, rt, t)


def body(dims, panel, trailing):
    frames = dims[0] * dims[1] * dims[2]
    rt, gram, cross = reduce_products(dims, panel, trailing)
    return finish(gram, cross, rt, trailing, gram.shape[0] // frames)


def solution(mesh):
    dims = (*frame_dims(mesh.shape["frames"]), mesh.shape["cols"])
    return jax.shard_map(
        functools.partial(body, dims),
        mesh=mesh,
        in_specs=(P("frames", "cols"), P("frames", "cols")),
        out_specs=(P("frames", None), P("frames", "cols"), P("frames", "cols")),
        check_vma=False,
    )
```

time: 603 us -> 99.1 us (0.16)
  waiting for transfers between devices: 398 us -> 0 us
  other arithmetic: 122 us -> 0 us
  Pallas kernels: 0 us -> 96 us
  starting transfers between devices: 30.6 us -> 0 us
  matrix products: 16.6 us -> 0 us
  between operations: 17.1 us -> 0.66 us
  local copies, waits for them, and re-layouts: 14.1 us -> 2.25 us
    psum x1 -> x0, waiting for transfers between devices: 194 us -> none  [body(): coupling = lax.psum(local_term, 'frames')]
    ppermute x6 -> x0, waiting for transfers between devices: 159 us -> none  [partner_2(): return lax.ppermute(value, axis, pairs)]
    another operation x17 -> x0, other arithmetic: 120 us -> none  [the longest x14 78.7 us: body(): lower = jnp.linalg.cholesky(gram)]
    pallas_call x0 -> x2, Pallas kernels: none -> 96 us  [the longest x1 66.9 us: reduce_products(): pl.pallas_call(functools.partial(reduce_kernel, dims), out_shape=(jax.Sha...]
    all_gather x1 -> x0, waiting for transfers between devices: 44.9 us -> none  [body(): row_block = lax.all_gather(panel, 'cols', axis=1, tiled=True)]
    ppermute x6 -> x0, starting transfers between devices: 30.5 us -> none  [partner_2(): return lax.ppermute(value, axis, pairs)]
    another operation x19 -> x0, local copies, waits for them, and re-layouts: 10.7 us -> none
    dot_general x3 -> x0, matrix products: 10.3 us -> none  [the longest x1 4.04 us: body(): jnp.dot(basis_t.T, coupling, precision=highest, preferred_element_type=jn...]
  transfers between devices with their start and end apart: 8 -> 0, of which waited for: 8 -> 0; matrix products, arithmetic and copies ran while one was open for 0% -> 0% of each run, Pallas kernels for 0% -> 0%
where the time goes in v1:
time: 99.1 us; the launch traced here: 98.9 us
  Pallas kernels  96 us (97%)
  local copies, waits for them, and re-layouts  2.25 us (2%)
    pallas_call x1, Pallas kernels, reduce_products(): pl.pallas_call(functools.partial(reduce_kernel, dims), out_shape=(jax.Sha...  66.9 us
    pallas_call x1, Pallas kernels, finish(): pl.pallas_call(functools.partial(finish_kernel, nb), out_shape=(jax.Shape...  29.1 us
    unnamed x5, local copies, waits for them, and re-layouts  2.25 us

profile of v1, /device:TPU:1, one launch (start us, length us, event | category | flops | bytes accessed | tf_op | source)
XLA Modules:
  0.0 98.9 jit_solution(14464895520753516926)
XLA Ops:
  0.6 1.0 %copy.5.panel_ref = f32[512,64]{1,0:T(8,128)S(1)} copy(f32[512,64]{0,1:T(8,128)} %param.2) | data formatting | bytes 262144 | tf_op args[0]
  1.7 0.0 copy-start
  1.7 1.2 %copy-done = f32[512,512]{1,0:T(8,128)S(1)} copy-done((f32[512,512]{1,0:T(8,128)S(1)}, f32[512,512]{1,0:T(8,128)}, u32[]{:S(2)}) %copy-start) | copy-done | bytes 1048600
  2.9 0.0 copy-start.1
  2.9 66.9 %reduce_products.1 = (f32[512,512]{1,0:T(8,128)S(1)}, f32[8,2,4,8,512]{4,3,2,1,0:T(8,128)S(1)}, f32[2,4,8,8,512]{4,3,2,1,0:T(8,128)S(1)}) custom-call(f32[512,64]{1,0:T(8,128)S(1)} %copy.5.panel_ref, f32[512,512]{1,0:T(8,128)S(1)} %copy-done), custom_call_target="tpu_custom_call" | custom-call | tf_op jit(solution)/shard_map/reduce_products/pallas_call | solution.py:168
  69.8 0.0 copy-done.1
  69.8 29.1 %finish.1 = (f32[8,512]{1,0:T(8,128)}, f32[8,512]{1,0:T(8,128)}, f32[512,512]{1,0:T(8,128)}) custom-call(f32[512,512]{1,0:T(8,128)S(1)} %bitcast.2, f32[512,512]{1,0:T(8,128)S(1)} %bitcast.3, f32[512,512]{1,0:T(8,128)S(1)} %get-tuple-element.8.rt_ref, f32[512,512]{1,0:T(8,128)S(1)} %copy-done.1), custom_call_target="tpu_custom_call" | custom-call | tf_op jit(solution)/shard_map/finish/pallas_call | solution.py:295
Async XLA Ops:
  1.7 1.2 %copy-start = (f32[512,512]{1,0:T(8,128)S(1)}, f32[512,512]{1,0:T(8,128)}, u32[]{:S(2)}) copy-start(f32[512,512]{1,0:T(8,128)} %t_ref.1) | copy-start | bytes 3145732
  2.9 66.9 %copy-start.1 = (f32[512,512]{1,0:T(8,128)S(1)}, f32[512,512]{1,0:T(8,128)}, u32[]{:S(2)}) copy-start(f32[512,512]{1,0:T(8,128)} %t_ref.1) | copy-start | bytes 3145732

commit v2 on v0

v2 whole, which is shorter than its diff:
```python
import functools

import jax
import jax.numpy as jnp
from jax import lax
from jax.experimental import pallas as pl
from jax.experimental.pallas import tpu as pltpu
from jax.sharding import PartitionSpec as P

HI = lax.Precision.HIGHEST
F32 = jnp.float32
BLOCK = 128
MESH = pl.DeviceIdType.MESH


def frame_dims(frames):
    return {64: (4, 8, 2), 8: (2, 2, 2)}[frames]


def sum_slots(ref):
    total = ref[0]
    for slot in range(1, ref.shape[0]):
        total = total + ref[slot]
    return total


def split3(v):
    h = v.astype(jnp.bfloat16).astype(F32)
    rest = v - h
    m = rest.astype(jnp.bfloat16).astype(F32)
    low = rest - m
    return h, m, low

def lane(v, c):
    return jnp.broadcast_to(v[:, c:c + 1], v.shape)

def factor_block(s_ref, m_ref):
    n = s_ref.shape[0]
    steps = n // 8
    sub = lax.broadcasted_iota(jnp.int32, (8, n), 0)
    col = lax.broadcasted_iota(jnp.int32, (8, n), 1)
    x = [jnp.broadcast_to(s_ref[i:i + 1, :], (8, n)) for i in range(8)]
    d = [[lane(x[i], k) for k in range(i + 1)] for i in range(8)]
    for j in range(steps):
        base = 8 * j
        own = (col >= base) & (col < base + 8)
        x = [jnp.where(own, jnp.where(col == base + i, 1.0, 0.0), x[i]) for i in range(8)]
        u = []
        low = [[None] * 8 for _ in range(8)]
        for k in range(8):
            scale = lax.rsqrt(d[k][k])
            for i in range(k + 1, 8):
                low[i][k] = d[i][k] * scale
            for i in range(k + 1, 8):
                for m in range(k + 1, i + 1):
                    d[i][m] = d[i][m] - low[i][k] * low[m][k]
            u.append(x[k] * scale)
            for i in range(k + 1, 8):
                x[i] = x[i] - low[i][k] * u[k]
        packed = u[7]
        for k in range(7):
            packed = jnp.where(sub == k, u[k], packed)
        m_ref[base:base + 8, :] = jnp.where(col < base + 8, packed, 0.0)
        if j == steps - 1:
            break
        nxt = base + 8
        if j + 2 < steps:
            h, mid, lo = split3(packed)
            left = jnp.concatenate([h, h, mid, mid, h, lo], axis=0).astype(jnp.bfloat16)
            right = jnp.concatenate([h, mid, h, mid, lo, h], axis=0).astype(jnp.bfloat16)
            update = lax.dot_general(left, right, (((0,), (0,)), ((), ())), preferred_element_type=F32)
        x = [jnp.broadcast_to(s_ref[nxt + i:nxt + i + 1, :], (8, n)) for i in range(8)]
        d = [[lane(x[i], nxt + k) for k in range(i + 1)] for i in range(8)]
        x = [jnp.where(own, 0.0, v) for v in x]
        for k in range(8):
            w = [lane(u[k], nxt + i) for i in range(8)]
            for i in range(8):
                x[i] = x[i] - w[i] * u[k]
                for m in range(i + 1):
                    d[i][m] = d[i][m] - w[i] * w[m]
        if j + 2 < steps:
            for p in range(j + 2, steps):
                s_ref[8 * p:8 * p + 8, :] = jnp.where(own, 0.0, s_ref[8 * p:8 * p + 8, :]) - update[8 * p:8 * p + 8, :]


def dot3(a, b, dims):
    ah, bh = a.astype(jnp.bfloat16), b.astype(jnp.bfloat16)
    al = (a - ah.astype(F32)).astype(jnp.bfloat16)
    bl = (b - bh.astype(F32)).astype(jnp.bfloat16)

    def one(u, v):
        return lax.dot_general(u, v, (dims, ((), ())), preferred_element_type=F32)

    return one(ah, bh) + (one(ah, bl) + one(al, bh))


def factor_step(step, b, s, v, r, blk, inv):
    n = s.shape[0]
    off = pl.multiple_of(step * b, b)
    wide = pl.ds(off, b)
    rowb = lax.broadcasted_iota(jnp.int32, (n, n), 0) // b
    colb = lax.broadcasted_iota(jnp.int32, (n, n), 1) // b
    col = lax.broadcasted_iota(jnp.int32, (b, n), 1)
    row = lax.broadcasted_iota(jnp.int32, (b, n), 0)
    blk[...] = s[wide, wide]
    factor_block(blk, inv)
    y = jnp.dot(inv[...], s[wide, :], precision=HI, preferred_element_type=F32)
    r[wide, :] = jnp.where(col >= row + off, y, 0.0)
    v[wide, :] = jnp.where(col < off, y, 0.0)
    v[wide, wide] = inv[...]
    coef = jnp.where(col >= off + b, y, 0.0)
    both = jnp.where(col >= off + b, y, v[wide, :])
    upd = lax.dot_general(coef, both, (((0,), (0,)), ((), ())), precision=HI, preferred_element_type=F32)
    s[...] = jnp.where((colb == step) & (rowb > step), 0.0, s[...]) - upd


def factor_kernel(
    dims, panel_ref, trail_hbm, rt_ref, c_ref, r_ref, v_ref,
    trail, gp, gcore, gs, gx, gy, g_ref, xs, xo, xcore, xx, xr, xy, s, blk, inv,
    load_sem, ring_send, ring_recv, core_send, core_recv, x_send, x_recv, y_send, y_recv, z_send, z_recv,
):
    nx, ny, nq, nz = dims
    f = lax.axis_index("frames")
    z = lax.axis_index("cols")
    q = lax.rem(f, nq)
    y = lax.rem(f // nq, ny)
    x = f // (nq * ny)
    xto = [lax.rem(x + d, nx) for d in range(nx)]
    yto = [lax.rem(y + d, ny) for d in range(ny)]
    zto = [lax.rem(z + d, nz) for d in range(nz)]
    other = lax.rem(q + 1, nq)

    def device(x=x, y=y, q=q, z=z):
        return ((x * ny + y) * nq + q, z)

    core = device(q=other)
    xdev = [device(x=to) for to in xto]
    ydev = [device(y=to) for to in yto]
    zdev = [device(z=to) for to in zto]
    load = pltpu.make_async_copy(trail_hbm, trail, load_sem)
    load.start()
    barrier = pltpu.get_barrier_semaphore()
    partners = [core] + xdev[1:] + ydev[1:] + zdev[1:]
    for to in partners:
        pl.semaphore_signal(barrier, inc=1, device_id=to, device_id_type=MESH)
    width = panel_ref.shape[0]
    rt_ref[pl.ds(pl.multiple_of(z * width, width), width), :] = panel_ref[...]
    pl.semaphore_wait(barrier, len(partners))

    pending = []

    def link(src, dst, send, recv, to):
        return pltpu.make_async_remote_copy(
            src_ref=src, dst_ref=dst, send_sem=send, recv_sem=recv, device_id=to, device_id_type=MESH
        )

    def push(copies):
        for copy in copies:
            copy.start()
            pending.append(copy)
        return copies

    def arrived(copies):
        for copy in copies:
            copy.wait_recv()

    def drain():
        for copy in pending:
            copy.wait_send()

    def along_core(stage, src, dst):
        return [link(src, dst, core_send.at[stage], core_recv.at[stage], core)]

    def along_x(stage, src, dst):
        return [
            link(src(xto[d]), dst, x_send.at[stage, d], x_recv.at[stage, d], xdev[d]) for d in range(1, nx)
        ]

    def along_y(stage, src, dst):
        return [
            link(src(yto[d]), dst, y_send.at[stage, d], y_recv.at[stage, d], ydev[d]) for d in range(1, ny)
        ]

    half = width // 2
    last = nz // 2 - 1
    moving = {}
    for hop in range(nz // 2):
        for piece in range(2):
            for way in range(2):
                if hop == last and piece != way:
                    continue
                if hop > 0:
                    moving[hop - 1, piece, way].wait_recv()
                owner, there = (zto[-hop], zdev[1]) if way == 0 else (zto[hop], zdev[-1])
                block = rt_ref.at[pl.ds(pl.multiple_of(owner * width + piece * half, half), half), :]
                copy = link(block, block, ring_send.at[way, hop, piece], ring_recv.at[way, hop, piece], there)
                moving[hop, piece, way] = copy
                push([copy])
    for key in moving:
        if (key[0] + 1, key[1], key[2]) not in moving:
            moving[key].wait_recv()

    g_core = along_core(0, gp.at[other], gcore)
    g_x = along_x(0, lambda to: gs.at[to], gx.at[x])
    g_y = along_y(0, lambda to: gy.at[y], gy.at[y])
    mine = g_ref.at[z, q, x]
    g_z = [link(mine, mine, z_send.at[d], z_recv.at[d], zdev[d]) for d in range(1, nz)]
    g_ax = along_x(2, lambda to: g_ref.at[:, q, x], g_ref.at[:, q, x])
    g_acore = along_core(2, g_ref.at[:, q], g_ref.at[:, q])
    x_core = along_core(1, xs, xcore)
    x_x = along_x(1, lambda to: xo.at[to], xx.at[x])
    x_y = along_y(1, lambda to: xr.at[to], xy.at[y])
    x_ay = along_y(2, lambda to: c_ref.at[q, x, y], c_ref.at[q, x, y])
    x_ax = along_x(3, lambda to: c_ref.at[q, x], c_ref.at[q, x])
    x_acore = along_core(3, c_ref.at[q], c_ref.at[q])
    rows = rt_ref.shape[0] // nq

    def cross(part):
        left = rt_ref[pl.ds(pl.multiple_of(part * rows, rows), rows), :]
        return dot3(left, trail[...], ((1,), (0,))).reshape(xs.shape)

    own = rt_ref[pl.ds(pl.multiple_of(z * width, width), width), :]
    gp[...] = lax.dot_general(
        own, rt_ref[...], (((1,), (1,)), ((), ())), precision=HI, preferred_element_type=F32
    ).reshape(gp.shape)
    push(g_core)
    load.wait()
    xs[...] = cross(other)
    push(x_core)
    arrived(g_core)
    gs[...] = gp[q] + gcore[...]
    gx[x] = gs[x]
    push(g_x)
    xo[...] = cross(q)
    arrived(x_core)
    xo[...] = xo[...] + xcore[...]
    xx[x] = xo[x]
    push(x_x)
    arrived(g_x)
    gy[y] = sum_slots(gx)
    push(g_y)
    arrived(g_y)
    g_ref[z, q, x] = sum_slots(gy)
    push(g_z)
    arrived(g_z)
    push(g_ax)
    arrived(x_x)
    xr[...] = sum_slots(xx)
    xy[y] = xr[y]
    push(x_y)
    arrived(g_ax)
    push(g_acore)
    arrived(x_y)
    c_ref[q, x, y] = sum_slots(xy)
    push(x_ay)
    arrived(g_acore)
    n = s.shape[0]
    s[...] = g_ref[...].reshape(n, n)
    b = blk.shape[0]

    @pl.loop(0, n // b)
    def _(block):
        factor_step(block, b, s, v_ref, r_ref, blk, inv)

        @pl.when(block == 0)
        def _():
            arrived(x_ay)
            push(x_ax)

        @pl.when(block == 2)
        def _():
            arrived(x_ax)
            push(x_acore)
    arrived(x_acore)
    drain()


def factor(dims, panel_t, trail):
    nx, ny, nq, nz = dims
    width, height = panel_t.shape
    cols = trail.shape[1]
    n = width * nz
    rg = n // (nz * nq * nx)
    rx = n // (nq * nx * ny)
    b = BLOCK
    vm = pl.BlockSpec(memory_space=pltpu.VMEM)
    dma = pltpu.SemaphoreType.DMA
    group = pltpu.VMEM((nx, rg, n), F32)
    half = pltpu.VMEM((nx, ny, rx, cols), F32)
    rt, c, r, v = pl.pallas_call(
        functools.partial(factor_kernel, dims),
        out_shape=(
            jax.ShapeDtypeStruct((n, height), F32),
            jax.ShapeDtypeStruct((nq, nx, ny, rx, cols), F32),
            jax.ShapeDtypeStruct((n, n), F32),
            jax.ShapeDtypeStruct((n, n), F32),
        ),
        in_specs=[vm, pl.BlockSpec(memory_space=pl.ANY)],
        out_specs=(vm,) * 4,
        scratch_shapes=[
            pltpu.VMEM(trail.shape, F32),
            pltpu.VMEM((nq, nx, rg, n), F32),
            group, group, group,
            pltpu.VMEM((ny, rg, n), F32),
            pltpu.VMEM((nz, nq, nx, rg, n), F32),
            half, half, half, half,
            pltpu.VMEM((ny, rx, cols), F32),
            pltpu.VMEM((ny, rx, cols), F32),
            pltpu.VMEM((n, n), F32),
            pltpu.VMEM((b, b), F32),
            pltpu.VMEM((b, b), F32),
            dma,
            dma((2, nz // 2, 2)), dma((2, nz // 2, 2)),
            dma((4,)), dma((4,)),
            dma((4, nx)), dma((4, nx)),
            dma((3, ny)), dma((3, ny)),
            dma((nz,)), dma((nz,)),
        ],
        compiler_params=pltpu.CompilerParams(
            collective_id=0, has_side_effects=True, vmem_limit_bytes=40 * 2**20
        ),
        name="factor",
    )(panel_t, trail)
    return rt, c.reshape(n, cols), r, v


def apply_kernel(c_ref, r_ref, v_ref, rt_ref, t_ref, r_out, c_out, rem_out, coup):
    coup[...] = dot3(v_ref[...], c_ref[...], ((1,), (0,)))
    basis_t = dot3(v_ref[...], rt_ref[...], ((1,), (0,)))
    rem_out[...] = t_ref[...] - dot3(basis_t, coup[...], ((0,), (0,)))
    height = r_out.shape[0]
    pos = pl.multiple_of(lax.axis_index("frames") * height, height)
    r_out[...] = r_ref[pl.ds(pos, height), :]
    c_out[...] = coup[pl.ds(pos, height), :]


def apply(c, r, v, rt, t, height):
    n, m = c.shape
    vm = pl.BlockSpec(memory_space=pltpu.VMEM)
    return pl.pallas_call(
        apply_kernel,
        out_shape=(
            jax.ShapeDtypeStruct((height, n), F32),
            jax.ShapeDtypeStruct((height, m), F32),
            jax.ShapeDtypeStruct(t.shape, F32),
        ),
        in_specs=[vm] * 5,
        out_specs=(vm,) * 3,
        scratch_shapes=[pltpu.VMEM((n, m), F32)],
        compiler_params=pltpu.CompilerParams(vmem_limit_bytes=40 * 2**20),
        name="apply",
    )(c, r, v, rt, t)


def body(dims, panel, trailing):
    frames = dims[0] * dims[1] * dims[2]
    rt, cross, r, v = factor(dims, panel.T, trailing)
    return apply(cross, r, v, rt, trailing, r.shape[0] // frames)


def solution(mesh):
    dims = (*frame_dims(mesh.shape["frames"]), mesh.shape["cols"])
    return jax.shard_map(
        functools.partial(body, dims),
        mesh=mesh,
        in_specs=(P("frames", "cols"), P("frames", "cols")),
        out_specs=(P("frames", None), P("frames", "cols"), P("frames", "cols")),
        check_vma=False,
    )
```

time: 603 us -> 89.2 us (0.15)
  waiting for transfers between devices: 398 us -> 0 us
  other arithmetic: 122 us -> 0 us
  Pallas kernels: 0 us -> 86.2 us
  starting transfers between devices: 30.6 us -> 0 us
  matrix products: 16.6 us -> 0 us
  between operations: 17.1 us -> 0.66 us
  local copies, waits for them, and re-layouts: 14.1 us -> 2.13 us
    psum x1 -> x0, waiting for transfers between devices: 194 us -> none  [body(): coupling = lax.psum(local_term, 'frames')]
    ppermute x6 -> x0, waiting for transfers between devices: 159 us -> none  [partner_2(): return lax.ppermute(value, axis, pairs)]
    another operation x17 -> x0, other arithmetic: 120 us -> none  [the longest x14 78.7 us: body(): lower = jnp.linalg.cholesky(gram)]
    pallas_call x0 -> x2, Pallas kernels: none -> 86.2 us  [the longest x1 82.5 us: factor(): pl.pallas_call(functools.partial(factor_kernel, dims), out_shape=(jax.Sha...]
    all_gather x1 -> x0, waiting for transfers between devices: 44.9 us -> none  [body(): row_block = lax.all_gather(panel, 'cols', axis=1, tiled=True)]
    ppermute x6 -> x0, starting transfers between devices: 30.5 us -> none  [partner_2(): return lax.ppermute(value, axis, pairs)]
    another operation x19 -> x0, local copies, waits for them, and re-layouts: 10.7 us -> none
    dot_general x3 -> x0, matrix products: 10.3 us -> none  [the longest x1 4.04 us: body(): jnp.dot(basis_t.T, coupling, precision=highest, preferred_element_type=jn...]
  transfers between devices with their start and end apart: 8 -> 0, of which waited for: 8 -> 0; matrix products, arithmetic and copies ran while one was open for 0% -> 0% of each run, Pallas kernels for 0% -> 0%
where the time goes in v2:
time: 89.2 us; the launch traced here: 89 us
  Pallas kernels  86.2 us (97%)
  local copies, waits for them, and re-layouts  2.13 us (2%)
    pallas_call x1, Pallas kernels, factor(): pl.pallas_call(functools.partial(factor_kernel, dims), out_shape=(jax.Sha...  82.5 us
    pallas_call x1, Pallas kernels, apply(): pl.pallas_call(apply_kernel, out_shape=(jax.ShapeDtypeStruct((height, n),...  3.72 us
    unnamed x6, local copies, waits for them, and re-layouts  2.13 us

profile of v2, /device:TPU:1, one launch (start us, length us, event | category | flops | bytes accessed | tf_op | source)
XLA Modules:
  0.0 89.0 jit_solution(4855938147326553743)
XLA Ops:
  0.6 0.0 copy-start
  0.6 1.2 %copy-done = f32[512,512]{1,0:T(8,128)S(1)} copy-done((f32[512,512]{1,0:T(8,128)S(1)}, f32[512,512]{1,0:T(8,128)}, u32[]{:S(2)}) %copy-start) | copy-done | bytes 1048600
  1.9 0.0 copy-start.2
  1.9 0.9 %copy-done.2 = f32[512,64]{0,1:T(8,128)S(1)} copy-done((f32[512,64]{0,1:T(8,128)S(1)}, f32[512,64]{0,1:T(8,128)}, u32[]{:S(2)}) %copy-start.2) | copy-done | bytes 131096
  2.8 0.0 copy-start.1
  2.8 82.5 %factor.1 = (f32[512,512]{1,0:T(8,128)S(1)}, f32[2,4,8,8,512]{4,3,2,1,0:T(8,128)S(1)}, f32[512,512]{1,0:T(8,128)S(1)}, f32[512,512]{1,0:T(8,128)S(1)}) custom-call(f32[64,512]{1,0:T(8,128)S(1)} %bitcast.3, f32[512,512]{1,0:T(8,128)S(1)} %copy-done), custom_call_target="tpu_custom_call" | custom-call | tf_op jit(solution)/shard_map/factor/pallas_call | solution.py:290
  85.3 0.0 copy-done.1
  85.3 3.7 %apply.1 = (f32[8,512]{1,0:T(8,128)}, f32[8,512]{1,0:T(8,128)}, f32[512,512]{1,0:T(8,128)}) custom-call(f32[512,512]{1,0:T(8,128)S(1)} %bitcast.2, f32[512,512]{1,0:T(8,128)S(1)} %get-tuple-element.8.r_ref, f32[512,512]{1,0:T(8,128)S(1)} %get-tuple-element.9.v_ref, f32[512,512]{1,0:T(8,128)S(1)} %get-tuple-element.10.rt_ref, f32[512,512]{1,0:T(8,128)S(1)} %copy-done.1), custom_call_target="tpu_custom_call" | custom-call | tf_op jit(solution)/shard_map/apply/pallas_call | solution.py:340
Async XLA Ops:
  0.6 1.2 %copy-start = (f32[512,512]{1,0:T(8,128)S(1)}, f32[512,512]{1,0:T(8,128)}, u32[]{:S(2)}) copy-start(f32[512,512]{1,0:T(8,128)} %t_ref.1) | copy-start | bytes 3145732
  1.9 0.9 %copy-start.2 = (f32[512,64]{0,1:T(8,128)S(1)}, f32[512,64]{0,1:T(8,128)}, u32[]{:S(2)}) copy-start(f32[512,64]{0,1:T(8,128)} %param.2) | copy-start | bytes 393220
  2.8 82.5 %copy-start.1 = (f32[512,512]{1,0:T(8,128)S(1)}, f32[512,512]{1,0:T(8,128)}, u32[]{:S(2)}) copy-start(f32[512,512]{1,0:T(8,128)} %t_ref.1) | copy-start | bytes 3145732

commit v3 on v2

--- a/solution.py
+++ b/solution.py
@@ -10,6 +10,7 @@
 HI = lax.Precision.HIGHEST
 F32 = jnp.float32
 BLOCK = 128
+PIECES = 4
 MESH = pl.DeviceIdType.MESH
 
 
@@ -69,15 +70,11 @@
             left = jnp.concatenate([h, h, mid, mid, h, lo], axis=0).astype(jnp.bfloat16)
             right = jnp.concatenate([h, mid, h, mid, lo, h], axis=0).astype(jnp.bfloat16)
             update = lax.dot_general(left, right, (((0,), (0,)), ((), ())), preferred_element_type=F32)
-        x = [jnp.broadcast_to(s_ref[nxt + i:nxt + i + 1, :], (8, n)) for i in range(8)]
-        d = [[lane(x[i], nxt + k) for k in range(i + 1)] for i in range(8)]
-        x = [jnp.where(own, 0.0, v) for v in x]
+        x = [jnp.where(own, 0.0, jnp.broadcast_to(s_ref[nxt + i:nxt + i + 1, :], (8, n))) for i in range(8)]
         for k in range(8):
-            w = [lane(u[k], nxt + i) for i in range(8)]
             for i in range(8):
-                x[i] = x[i] - w[i] * u[k]
-                for m in range(i + 1):
-                    d[i][m] = d[i][m] - w[i] * w[m]
+                x[i] = x[i] - lane(u[k], nxt + i) * u[k]
+        d = [[lane(x[i], nxt + m) for m in range(i + 1)] for i in range(8)]
         if j + 2 < steps:
             for p in range(j + 2, steps):
                 s_ref[8 * p:8 * p + 8, :] = jnp.where(own, 0.0, s_ref[8 * p:8 * p + 8, :]) - update[8 * p:8 * p + 8, :]
@@ -108,16 +105,20 @@
     r[wide, :] = jnp.where(col >= row + off, y, 0.0)
     v[wide, :] = jnp.where(col < off, y, 0.0)
     v[wide, wide] = inv[...]
-    coef = jnp.where(col >= off + b, y, 0.0)
-    both = jnp.where(col >= off + b, y, v[wide, :])
-    upd = lax.dot_general(coef, both, (((0,), (0,)), ((), ())), precision=HI, preferred_element_type=F32)
-    s[...] = jnp.where((colb == step) & (rowb > step), 0.0, s[...]) - upd
+
+    @pl.when(off + b < n)
+    def _():
+        coef = jnp.where(col >= off + b, y, 0.0)
+        both = jnp.where(col >= off + b, y, v[wide, :])
+        upd = lax.dot_general(coef, both, (((0,), (0,)), ((), ())), precision=HI, preferred_element_type=F32)
+        s[...] = jnp.where((colb == step) & (rowb > step), 0.0, s[...]) - upd
 
 
 def factor_kernel(
-    dims, panel_ref, trail_hbm, rt_ref, c_ref, r_ref, v_ref,
-    trail, gp, gcore, gs, gx, gy, g_ref, xs, xo, xcore, xx, xr, xy, s, blk, inv,
+    dims, panel_hbm, trail_hbm, rt_ref, c_ref, r_ref, v_ref, trail,
+    gp, gcore, gs, gx, gy, g_ref, xs, xo, xcore, xx, xr, xy, s, blk, inv,
     load_sem, ring_send, ring_recv, core_send, core_recv, x_send, x_recv, y_send, y_recv, z_send, z_recv,
+    gx_send, gx_recv, gc_send, gc_recv,
 ):
     nx, ny, nq, nz = dims
     f = lax.axis_index("frames")
@@ -137,14 +138,17 @@
     xdev = [device(x=to) for to in xto]
     ydev = [device(y=to) for to in yto]
     zdev = [device(z=to) for to in zto]
-    load = pltpu.make_async_copy(trail_hbm, trail, load_sem)
+    width = panel_hbm.shape[0]
+    mine = rt_ref.at[pl.ds(pl.multiple_of(z * width, width), width), :]
+    fetch = pltpu.make_async_copy(panel_hbm, mine, load_sem.at[0])
+    fetch.start()
+    load = pltpu.make_async_copy(trail_hbm, trail, load_sem.at[1])
     load.start()
     barrier = pltpu.get_barrier_semaphore()
     partners = [core] + xdev[1:] + ydev[1:] + zdev[1:]
     for to in partners:
         pl.semaphore_signal(barrier, inc=1, device_id=to, device_id_type=MESH)
-    width = panel_ref.shape[0]
-    rt_ref[pl.ds(pl.multiple_of(z * width, width), width), :] = panel_ref[...]
+    fetch.wait()
     pl.semaphore_wait(barrier, len(partners))
 
     pending = []
@@ -181,18 +185,18 @@
             link(src(yto[d]), dst, y_send.at[stage, d], y_recv.at[stage, d], ydev[d]) for d in range(1, ny)
         ]
 
-    half = width // 2
+    part = width // PIECES
     last = nz // 2 - 1
     moving = {}
     for hop in range(nz // 2):
-        for piece in range(2):
+        for piece in range(PIECES):
             for way in range(2):
-                if hop == last and piece != way:
+                if hop == last and piece % 2 != way:
                     continue
                 if hop > 0:
                     moving[hop - 1, piece, way].wait_recv()
                 owner, there = (zto[-hop], zdev[1]) if way == 0 else (zto[hop], zdev[-1])
-                block = rt_ref.at[pl.ds(pl.multiple_of(owner * width + piece * half, half), half), :]
+                block = rt_ref.at[pl.ds(pl.multiple_of(owner * width + piece * part, part), part), :]
                 copy = link(block, block, ring_send.at[way, hop, piece], ring_recv.at[way, hop, piece], there)
                 moving[hop, piece, way] = copy
                 push([copy])
@@ -203,10 +207,18 @@
     g_core = along_core(0, gp.at[other], gcore)
     g_x = along_x(0, lambda to: gs.at[to], gx.at[x])
     g_y = along_y(0, lambda to: gy.at[y], gy.at[y])
-    mine = g_ref.at[z, q, x]
-    g_z = [link(mine, mine, z_send.at[d], z_recv.at[d], zdev[d]) for d in range(1, nz)]
-    g_ax = along_x(2, lambda to: g_ref.at[:, q, x], g_ref.at[:, q, x])
-    g_acore = along_core(2, g_ref.at[:, q], g_ref.at[:, q])
+    near_z = sorted(range(nz), key=lambda d: min(d, nz - d))
+    near_x = sorted(range(1, nx), key=lambda d: min(d, nx - d))
+    rows_g = {(dz, dx): g_ref.at[zto[-dz], q, xto[-dx]] for dz in range(nz) for dx in range(nx)}
+    g_z = {d: link(rows_g[0, 0], rows_g[0, 0], z_send.at[d], z_recv.at[d], zdev[d]) for d in range(1, nz)}
+    g_ax = {
+        (dz, dx): link(rows_g[dz, 0], rows_g[dz, 0], gx_send.at[dz, dx], gx_recv.at[dz, dx], xdev[dx])
+        for dz in range(nz)
+        for dx in range(1, nx)
+    }
+    g_ac = {
+        key: link(rows_g[key], rows_g[key], gc_send.at[key], gc_recv.at[key], core) for key in rows_g
+    }
     x_core = along_core(1, xs, xcore)
     x_x = along_x(1, lambda to: xo.at[to], xx.at[x])
     x_y = along_y(1, lambda to: xr.at[to], xy.at[y])
@@ -241,19 +253,24 @@
     push(g_y)
     arrived(g_y)
     g_ref[z, q, x] = sum_slots(gy)
-    push(g_z)
-    arrived(g_z)
-    push(g_ax)
+    push([g_z[d] for d in reversed(near_z[1:])])
+    for dz in near_z:
+        if dz > 0:
+            arrived([g_z[dz]])
+        push([g_ax[dz, dx] for dx in near_x])
+        push([g_ac[dz, 0]])
     arrived(x_x)
     xr[...] = sum_slots(xx)
     xy[y] = xr[y]
     push(x_y)
-    arrived(g_ax)
-    push(g_acore)
+    for dz in near_z:
+        for dx in near_x:
+            arrived([g_ax[dz, dx]])
+            push([g_ac[dz, dx]])
     arrived(x_y)
     c_ref[q, x, y] = sum_slots(xy)
     push(x_ay)
-    arrived(g_acore)
+    arrived(g_ac.values())
     n = s.shape[0]
     s[...] = g_ref[...].reshape(n, n)
     b = blk.shape[0]
@@ -273,6 +290,10 @@
             push(x_acore)
     arrived(x_acore)
     drain()
+
+
+def in_hbm(array):
+    return pltpu.with_memory_space_constraint(array, pltpu.HBM)
 
 
 def factor(dims, panel_t, trail):
@@ -287,18 +308,18 @@
     dma = pltpu.SemaphoreType.DMA
     group = pltpu.VMEM((nx, rg, n), F32)
     half = pltpu.VMEM((nx, ny, rx, cols), F32)
-    rt, c, r, v = pl.pallas_call(
+    rt, c, r, v, t = pl.pallas_call(
         functools.partial(factor_kernel, dims),
         out_shape=(
             jax.ShapeDtypeStruct((n, height), F32),
             jax.ShapeDtypeStruct((nq, nx, ny, rx, cols), F32),
             jax.ShapeDtypeStruct((n, n), F32),
             jax.ShapeDtypeStruct((n, n), F32),
+            jax.ShapeDtypeStruct(trail.shape, F32),
         ),
-        in_specs=[vm, pl.BlockSpec(memory_space=pl.ANY)],
-        out_specs=(vm,) * 4,
+        in_specs=[pl.BlockSpec(memory_space=pltpu.HBM)] * 2,
+        out_specs=(vm,) * 5,
         scratch_shapes=[
-            pltpu.VMEM(trail.shape, F32),
             pltpu.VMEM((nq, nx, rg, n), F32),
             group, group, group,
             pltpu.VMEM((ny, rg, n), F32),
@@ -309,19 +330,21 @@
             pltpu.VMEM((n, n), F32),
             pltpu.VMEM((b, b), F32),
             pltpu.VMEM((b, b), F32),
-            dma,
-            dma((2, nz // 2, 2)), dma((2, nz // 2, 2)),
+            dma((2,)),
+            dma((2, nz // 2, PIECES)), dma((2, nz // 2, PIECES)),
             dma((4,)), dma((4,)),
             dma((4, nx)), dma((4, nx)),
             dma((3, ny)), dma((3, ny)),
             dma((nz,)), dma((nz,)),
+            dma((nz, nx)), dma((nz, nx)),
+            dma((nz, nx)), dma((nz, nx)),
         ],
         compiler_params=pltpu.CompilerParams(
             collective_id=0, has_side_effects=True, vmem_limit_bytes=40 * 2**20
         ),
         name="factor",
-    )(panel_t, trail)
-    return rt, c.reshape(n, cols), r, v
+    )(in_hbm(panel_t), in_hbm(trail))
+    return rt, c.reshape(n, cols), r, v, t
 
 
 def apply_kernel(c_ref, r_ref, v_ref, rt_ref, t_ref, r_out, c_out, rem_out, coup):
@@ -354,8 +377,8 @@
 
 def body(dims, panel, trailing):
     frames = dims[0] * dims[1] * dims[2]
-    rt, cross, r, v = factor(dims, panel.T, trailing)
-    return apply(cross, r, v, rt, trailing, r.shape[0] // frames)
+    rt, cross, r, v, t = factor(dims, panel.T, trailing)
+    return apply(cross, r, v, rt, t, r.shape[0] // frames)
 
 
 def solution(mesh):

time: 89.2 us -> 82.5 us (0.925)
  Pallas kernels: 86.2 us -> 81.7 us
  local copies, waits for them, and re-layouts: 2.13 us -> 0 us
    pallas_call x1, Pallas kernels: 82.5 us -> 78 us  [factor(): pl.pallas_call(functools.partial(factor_kernel, dims), out_shape=(jax.Sha...]
    unnamed x6 -> x0, local copies, waits for them, and re-layouts: 2.13 us -> none
where the time goes in v3:
time: 82.5 us; the launch traced here: 82.3 us
  Pallas kernels  81.7 us (99%)
    pallas_call x1, Pallas kernels, factor(): pl.pallas_call(functools.partial(factor_kernel, dims), out_shape=(jax.Sha...  78 us
    pallas_call x1, Pallas kernels, apply(): pl.pallas_call(apply_kernel, out_shape=(jax.ShapeDtypeStruct((height, n),...  3.72 us

profile of v3, /device:TPU:1, one launch (start us, length us, event | category | flops | bytes accessed | tf_op | source)
XLA Modules:
  0.0 82.3 jit_solution(2490623365804234873)
XLA Ops:
  0.6 78.0 %factor.1 = (f32[512,512]{1,0:T(8,128)S(1)}, f32[2,4,8,8,512]{4,3,2,1,0:T(8,128)S(1)}, f32[512,512]{1,0:T(8,128)S(1)}, f32[512,512]{1,0:T(8,128)S(1)}, f32[512,512]{1,0:T(8,128)S(1)}) custom-call(f32[64,512]{1,0:T(8,128)} %bitcast.3, f32[512,512]{1,0:T(8,128)} %trail_hbm.1), custom_call_target="tpu_custom_call" | custom-call | tf_op jit(solution)/shard_map/factor/pallas_call | solution.py:311
  78.6 3.7 %apply.1 = (f32[8,512]{1,0:T(8,128)}, f32[8,512]{1,0:T(8,128)}, f32[512,512]{1,0:T(8,128)}) custom-call(f32[512,512]{1,0:T(8,128)S(1)} %bitcast.2, f32[512,512]{1,0:T(8,128)S(1)} %get-tuple-element.9.r_ref, f32[512,512]{1,0:T(8,128)S(1)} %get-tuple-element.10.v_ref, f32[512,512]{1,0:T(8,128)S(1)} %get-tuple-element.11.rt_ref, ...), custom_call_target="tpu_custom_call" | custom-call | tf_op jit(solution)/shard_map/apply/pallas_call | solution.py:363

commit v4 on v3

--- a/solution.py
+++ b/solution.py
@@ -35,7 +35,11 @@
 def lane(v, c):
     return jnp.broadcast_to(v[:, c:c + 1], v.shape)
 
-def factor_block(s_ref, m_ref):
+EARLY = 0
+GROUPS = ((0, 1, 2, 3), (4, 5), (6,), (7,))
+
+
+def factor_block(s_ref, m_ref, w_ref):
     n = s_ref.shape[0]
     steps = n // 8
     sub = lax.broadcasted_iota(jnp.int32, (8, n), 0)
@@ -65,18 +69,49 @@
         if j == steps - 1:
             break
         nxt = base + 8
-        if j + 2 < steps:
+        if j + 3 < steps:
             h, mid, lo = split3(packed)
             left = jnp.concatenate([h, h, mid, mid, h, lo], axis=0).astype(jnp.bfloat16)
             right = jnp.concatenate([h, mid, h, mid, lo, h], axis=0).astype(jnp.bfloat16)
             update = lax.dot_general(left, right, (((0,), (0,)), ((), ())), preferred_element_type=F32)
-        x = [jnp.where(own, 0.0, jnp.broadcast_to(s_ref[nxt + i:nxt + i + 1, :], (8, n))) for i in range(8)]
-        for k in range(8):
-            for i in range(8):
-                x[i] = x[i] - lane(u[k], nxt + i) * u[k]
-        d = [[lane(x[i], nxt + m) for m in range(i + 1)] for i in range(8)]
+
+        def below(rows_at, y, groups, first, early=0):
+            for slot, group in enumerate(groups, first):
+                if len(group) == 1:
+                    w = {(group[0], i): lane(u[group[0]], rows_at + i) for i in range(8)}
+                else:
+                    some = u[group[-1]]
+                    for k in group[:-1]:
+                        some = jnp.where(sub == k, u[k], some)
+                    for i in range(8):
+                        w_ref[j % 2, slot, i] = lane(some, rows_at + i)
+                    w = {
+                        (k, i): jnp.broadcast_to(w_ref[j % 2, slot, i, k:k + 1, :], (8, n))
+                        for k in group
+                        for i in range(8)
+                    }
+                for k in group:
+                    for i in range(8):
+                        y[i] = y[i] - w[k, i] * u[k]
+                        for m in range(min(early, i + 1)):
+                            d[i][m] = d[i][m] - w[k, i] * w[k, m]
+            return y
+
+        def rows_of(at):
+            return [jnp.broadcast_to(s_ref[at + i:at + i + 1, :], (8, n)) for i in range(8)]
+
+        x = ahead if j > 0 else rows_of(nxt)
+        d = [[lane(x[i], nxt + m) if m < EARLY else None for m in range(i + 1)] for i in range(8)]
+        x = [jnp.where(own, 0.0, v) for v in x]
+        x = below(nxt, x, GROUPS, 0, EARLY)
+        for i in range(8):
+            for m in range(EARLY, i + 1):
+                d[i][m] = lane(x[i], nxt + m)
         if j + 2 < steps:
-            for p in range(j + 2, steps):
+            ahead = [jnp.where(own, 0.0, v) for v in rows_of(nxt + 8)]
+            ahead = below(nxt + 8, ahead, (tuple(range(8)),), len(GROUPS))
+        if j + 3 < steps:
+            for p in range(j + 3, steps):
                 s_ref[8 * p:8 * p + 8, :] = jnp.where(own, 0.0, s_ref[8 * p:8 * p + 8, :]) - update[8 * p:8 * p + 8, :]
 
 
@@ -91,32 +126,42 @@
     return one(ah, bh) + (one(ah, bl) + one(al, bh))
 
 
-def factor_step(step, b, s, v, r, blk, inv):
+def factor_step(step, b, s, v, r, blk, inv, wide_ref):
     n = s.shape[0]
-    off = pl.multiple_of(step * b, b)
-    wide = pl.ds(off, b)
-    rowb = lax.broadcasted_iota(jnp.int32, (n, n), 0) // b
-    colb = lax.broadcasted_iota(jnp.int32, (n, n), 1) // b
-    col = lax.broadcasted_iota(jnp.int32, (b, n), 1)
-    row = lax.broadcasted_iota(jnp.int32, (b, n), 0)
-    blk[...] = s[wide, wide]
-    factor_block(blk, inv)
-    y = jnp.dot(inv[...], s[wide, :], precision=HI, preferred_element_type=F32)
-    r[wide, :] = jnp.where(col >= row + off, y, 0.0)
-    v[wide, :] = jnp.where(col < off, y, 0.0)
-    v[wide, wide] = inv[...]
-
-    @pl.when(off + b < n)
-    def _():
-        coef = jnp.where(col >= off + b, y, 0.0)
-        both = jnp.where(col >= off + b, y, v[wide, :])
-        upd = lax.dot_general(coef, both, (((0,), (0,)), ((), ())), precision=HI, preferred_element_type=F32)
-        s[...] = jnp.where((colb == step) & (rowb > step), 0.0, s[...]) - upd
+    off = step * b
+    end = off + b
+    blk[...] = s[off:end, off:end]
+    factor_block(blk, inv, wide_ref)
+    y = jnp.dot(inv[...], s[off:end, :], precision=HI, preferred_element_type=F32)
+    col = lax.broadcasted_iota(jnp.int32, (b, b), 1)
+    row = lax.broadcasted_iota(jnp.int32, (b, b), 0)
+    r[off:end, off:end] = jnp.where(col >= row, y[:, off:end], 0.0)
+    v[off:end, off:end] = inv[...]
+    if off > 0:
+        r[off:end, :off] = jnp.zeros((b, off), F32)
+        v[off:end, :off] = y[:, :off]
+    if end < n:
+        right = y[:, end:]
+        r[off:end, end:] = right
+        v[off:end, end:] = jnp.zeros((b, n - end), F32)
+
+        def take(lo, hi, coef, part, fresh):
+            upd = lax.dot_general(coef, part, (((0,), (0,)), ((), ())), precision=HI, preferred_element_type=F32)
+            s[end:, lo:hi] = -upd if fresh else s[end:, lo:hi] - upd
+
+        take(end, n, right, right, False)
+        take(off, end, right, inv[...], True)
+        if off > 0:
+            take(0, off, right, y[:, :off], False)
+
+
+def far_first(n):
+    return sorted(range(1, n), key=lambda d: -min(d, n - d))
 
 
 def factor_kernel(
     dims, panel_hbm, trail_hbm, rt_ref, c_ref, r_ref, v_ref, trail,
-    gp, gcore, gs, gx, gy, g_ref, xs, xo, xcore, xx, xr, xy, s, blk, inv,
+    gp, gcore, gs, gx, gy, g_ref, xs, xo, xcore, xx, xr, xy, s, blk, inv, wide,
     load_sem, ring_send, ring_recv, core_send, core_recv, x_send, x_recv, y_send, y_recv, z_send, z_recv,
     gx_send, gx_recv, gc_send, gc_recv,
 ):
@@ -177,12 +222,12 @@
 
     def along_x(stage, src, dst):
         return [
-            link(src(xto[d]), dst, x_send.at[stage, d], x_recv.at[stage, d], xdev[d]) for d in range(1, nx)
+            link(src(xto[d]), dst, x_send.at[stage, d], x_recv.at[stage, d], xdev[d]) for d in far_first(nx)
         ]
 
     def along_y(stage, src, dst):
         return [
-            link(src(yto[d]), dst, y_send.at[stage, d], y_recv.at[stage, d], ydev[d]) for d in range(1, ny)
+            link(src(yto[d]), dst, y_send.at[stage, d], y_recv.at[stage, d], ydev[d]) for d in far_first(ny)
         ]
 
     part = width // PIECES
@@ -253,7 +298,7 @@
     push(g_y)
     arrived(g_y)
     g_ref[z, q, x] = sum_slots(gy)
-    push([g_z[d] for d in reversed(near_z[1:])])
+    push([g_z[d] for d in far_first(nz)])
     for dz in near_z:
         if dz > 0:
             arrived([g_z[dz]])
@@ -275,17 +320,12 @@
     s[...] = g_ref[...].reshape(n, n)
     b = blk.shape[0]
 
-    @pl.loop(0, n // b)
-    def _(block):
-        factor_step(block, b, s, v_ref, r_ref, blk, inv)
-
-        @pl.when(block == 0)
-        def _():
+    for block in range(n // b):
+        factor_step(block, b, s, v_ref, r_ref, blk, inv, wide)
+        if block == 0:
             arrived(x_ay)
             push(x_ax)
-
-        @pl.when(block == 2)
-        def _():
+        if block == n // b - 2:
             arrived(x_ax)
             push(x_acore)
     arrived(x_acore)
@@ -330,6 +370,7 @@
             pltpu.VMEM((n, n), F32),
             pltpu.VMEM((b, b), F32),
             pltpu.VMEM((b, b), F32),
+            pltpu.VMEM((2, 8, 8, 8, b), F32),
             dma((2,)),
             dma((2, nz // 2, PIECES)), dma((2, nz // 2, PIECES)),
             dma((4,)), dma((4,)),

time: 82.5 us -> 80.8 us (0.979)
  Pallas kernels: 81.7 us -> 80 us
    pallas_call x1, Pallas kernels: 78 us -> 76.3 us  [factor(): pl.pallas_call(functools.partial(factor_kernel, dims), out_shape=(jax.Sha...]
where the time goes in v4:
time: 80.8 us; the launch traced here: 80.6 us
  Pallas kernels  80 us (99%)
    pallas_call x1, Pallas kernels, factor(): pl.pallas_call(functools.partial(factor_kernel, dims), out_shape=(jax.Sha...  76.3 us
    pallas_call x1, Pallas kernels, apply(): pl.pallas_call(apply_kernel, out_shape=(jax.ShapeDtypeStruct((height, n),...  3.72 us

profile of v4, /device:TPU:1, one launch (start us, length us, event | category | flops | bytes accessed | tf_op | source)
XLA Modules:
  0.0 80.6 jit_solution(3315085632324145170)
XLA Ops:
  0.6 76.3 %factor.1 = (f32[512,512]{1,0:T(8,128)S(1)}, f32[2,4,8,8,512]{4,3,2,1,0:T(8,128)S(1)}, f32[512,512]{1,0:T(8,128)S(1)}, f32[512,512]{1,0:T(8,128)S(1)}, f32[512,512]{1,0:T(8,128)S(1)}) custom-call(f32[64,512]{1,0:T(8,128)} %bitcast.3, f32[512,512]{1,0:T(8,128)} %trail_hbm.1), custom_call_target="tpu_custom_call" | custom-call | tf_op jit(solution)/shard_map/factor/pallas_call | solution.py:351
  76.9 3.7 %apply.1 = (f32[8,512]{1,0:T(8,128)}, f32[8,512]{1,0:T(8,128)}, f32[512,512]{1,0:T(8,128)}) custom-call(f32[512,512]{1,0:T(8,128)S(1)} %bitcast.2, f32[512,512]{1,0:T(8,128)S(1)} %get-tuple-element.9.r_ref, f32[512,512]{1,0:T(8,128)S(1)} %get-tuple-element.10.v_ref, f32[512,512]{1,0:T(8,128)S(1)} %get-tuple-element.11.rt_ref, ...), custom_call_target="tpu_custom_call" | custom-call | tf_op jit(solution)/shard_map/apply/pallas_call | solution.py:404

commit v5 on v4

--- a/solution.py
+++ b/solution.py
@@ -130,8 +130,9 @@
     n = s.shape[0]
     off = step * b
     end = off + b
-    blk[...] = s[off:end, off:end]
-    factor_block(blk, inv, wide_ref)
+    if off > 0:
+        blk[...] = s[off:end, off:end]
+        factor_block(blk, inv, wide_ref)
     y = jnp.dot(inv[...], s[off:end, :], precision=HI, preferred_element_type=F32)
     col = lax.broadcasted_iota(jnp.int32, (b, b), 1)
     row = lax.broadcasted_iota(jnp.int32, (b, b), 0)
@@ -252,10 +253,11 @@
     g_core = along_core(0, gp.at[other], gcore)
     g_x = along_x(0, lambda to: gs.at[to], gx.at[x])
     g_y = along_y(0, lambda to: gy.at[y], gy.at[y])
-    near_z = sorted(range(nz), key=lambda d: min(d, nz - d))
     near_x = sorted(range(1, nx), key=lambda d: min(d, nx - d))
-    rows_g = {(dz, dx): g_ref.at[zto[-dz], q, xto[-dx]] for dz in range(nz) for dx in range(nx)}
-    g_z = {d: link(rows_g[0, 0], rows_g[0, 0], z_send.at[d], z_recv.at[d], zdev[d]) for d in range(1, nz)}
+    rows_g = {(dz, dx): g_ref.at[dz, q, xto[-dx]] for dz in range(nz) for dx in range(nx)}
+    mine = g_ref.at[z, q, x]
+    g_z = [link(mine, mine, z_send.at[d], z_recv.at[z], zdev[d]) for d in far_first(nz)]
+    from_z = [link(rows_g[at, 0], rows_g[at, 0], z_send.at[0], z_recv.at[at], core) for at in range(nz)]
     g_ax = {
         (dz, dx): link(rows_g[dz, 0], rows_g[dz, 0], gx_send.at[dz, dx], gx_recv.at[dz, dx], xdev[dx])
         for dz in range(nz)
@@ -298,27 +300,35 @@
     push(g_y)
     arrived(g_y)
     g_ref[z, q, x] = sum_slots(gy)
-    push([g_z[d] for d in far_first(nz)])
-    for dz in near_z:
-        if dz > 0:
-            arrived([g_z[dz]])
+    push(g_z)
+    for dz in range(nz):
+
+        @pl.when(z != dz)
+        def _():
+            from_z[dz].wait_recv()
+
         push([g_ax[dz, dx] for dx in near_x])
         push([g_ac[dz, 0]])
     arrived(x_x)
     xr[...] = sum_slots(xx)
     xy[y] = xr[y]
     push(x_y)
-    for dz in near_z:
+    for dz in range(nz):
         for dx in near_x:
             arrived([g_ax[dz, dx]])
             push([g_ac[dz, dx]])
     arrived(x_y)
     c_ref[q, x, y] = sum_slots(xy)
     push(x_ay)
-    arrived(g_ac.values())
     n = s.shape[0]
-    s[...] = g_ref[...].reshape(n, n)
     b = blk.shape[0]
+    early = nz * b // n
+    arrived([g_ac[key] for key in g_ac if key[0] < early])
+    s[:b, :] = g_ref[:early].reshape(b, n)
+    blk[...] = s[:b, :b]
+    factor_block(blk, inv, wide)
+    arrived([g_ac[key] for key in g_ac if key[0] >= early])
+    s[b:, :] = g_ref[early:].reshape(n - b, n)
 
     for block in range(n // b):
         factor_step(block, b, s, v_ref, r_ref, blk, inv, wide)

time: 80.8 us -> 78.2 us (0.968)
  Pallas kernels: 80 us -> 76.9 us
    pallas_call x1, Pallas kernels: 76.3 us -> 73.2 us  [factor(): pl.pallas_call(functools.partial(factor_kernel, dims), out_shape=(jax.Sha...]
where the time goes in v5:
time: 78.2 us; the launch traced here: 77.5 us
  Pallas kernels  76.9 us (98%)
    pallas_call x1, Pallas kernels, factor(): pl.pallas_call(functools.partial(factor_kernel, dims), out_shape=(jax.Sha...  73.2 us
    pallas_call x1, Pallas kernels, apply(): pl.pallas_call(apply_kernel, out_shape=(jax.ShapeDtypeStruct((height, n),...  3.72 us

profile of v5, /device:TPU:1, one launch (start us, length us, event | category | flops | bytes accessed | tf_op | source)
XLA Modules:
  0.0 77.5 jit_solution(6691573297184395291)
XLA Ops:
  0.6 73.2 %factor.1 = (f32[512,512]{1,0:T(8,128)S(1)}, f32[2,4,8,8,512]{4,3,2,1,0:T(8,128)S(1)}, f32[512,512]{1,0:T(8,128)S(1)}, f32[512,512]{1,0:T(8,128)S(1)}, f32[512,512]{1,0:T(8,128)S(1)}) custom-call(f32[64,512]{1,0:T(8,128)} %bitcast.3, f32[512,512]{1,0:T(8,128)} %trail_hbm.1), custom_call_target="tpu_custom_call" | custom-call | tf_op jit(solution)/shard_map/factor/pallas_call | solution.py:361
  73.8 3.7 %apply.1 = (f32[8,512]{1,0:T(8,128)}, f32[8,512]{1,0:T(8,128)}, f32[512,512]{1,0:T(8,128)}) custom-call(f32[512,512]{1,0:T(8,128)S(1)} %bitcast.2, f32[512,512]{1,0:T(8,128)S(1)} %get-tuple-element.9.r_ref, f32[512,512]{1,0:T(8,128)S(1)} %get-tuple-element.10.v_ref, f32[512,512]{1,0:T(8,128)S(1)} %get-tuple-element.11.rt_ref, ...), custom_call_target="tpu_custom_call" | custom-call | tf_op jit(solution)/shard_map/apply/pallas_call | solution.py:414
